TPU v7x, 256 devices: a whole 4x4x8 slice. The times are simulated.
256 devices in a mesh: aux: 2 (over core), row: 8 (over z), col: 16 (over x, y).
Axes of the slice: x: 4, y: 4, z: 8, core: 2. Of those that a mesh axis runs over, the one named last changes fastest.
Arguments:
- coulomb: bfloat16 [64, 2048, 2048], P('aux', 'row', 'col'), may hold values from -6 to 6
- occupied: bfloat16 [2048, 2048], P('row'), may hold values from -0.125 to 0.125
- virtual: bfloat16 [2048, 2048], P('row'), may hold values from -0.125 to 0.125
- tile_mask: int32 [16, 16], replicated, may hold values 0 or 1
Outputs:
- chi: float32 [64, 64], P('aux')
All inputs are finite; a program needn't handle non-finite values.
Results may differ from a plain program's by a relative error of at most 0.0042.
Values may be sent and summed in bfloat16 or wider, within the bound.
A program may use at most 128 MiB of HBM per device.

v0:
```python
import jax
import jax.numpy as jnp
from jax import lax
from jax.sharding import PartitionSpec as P

NAO = 2048
TILE = 128


def swapped(value, axis, apart):
    mask = 2**apart
    pairs = [(source, source ^ mask) for source in range(lax.axis_size(axis))]
    return lax.ppermute(value, axis, pairs)


def shards(coulomb, occupied, virtual, tile_mask):
    rows = lax.axis_size("row")
    cols = lax.axis_size("col")
    pdev, mrow, ncol = coulomb.shape
    nao = mrow * rows
    row_idx = lax.axis_index("row")
    col_idx = lax.axis_index("col")
    aux_idx = lax.axis_index("aux")
    tiles_r = mrow // TILE
    tiles_c = ncol // TILE
    local_tiles = lax.dynamic_slice(
        tile_mask, (row_idx * tiles_r, col_idx * tiles_c), (tiles_r, tiles_c)
    )
    local_mask = jnp.repeat(jnp.repeat(local_tiles, TILE, axis=0), TILE, axis=1).astype(
        jnp.bfloat16
    )
    screened = coulomb * local_mask[None]
    moved = lax.all_to_all(screened, "row", split_axis=0, concat_axis=1, tiled=True)
    pieces = moved.shape[0]
    occ_all, virt_all = (
        lax.all_gather(occupied, "row", axis=0, tiled=True),
        lax.all_gather(virtual, "row", axis=0, tiled=True),
    )
    half = jnp.einsum("ml,pmn->pln", occ_all, moved, preferred_element_type=jnp.float32).astype(
        jnp.bfloat16
    )
    jpart = mrow // cols
    shaped = half.reshape(pieces, rows, cols, jpart, ncol)
    spread = lax.all_to_all(shaped, "col", split_axis=2, concat_axis=4, tiled=True)
    spread = spread.reshape(pieces, rows * jpart, nao)
    dressed = jnp.einsum(
        "pln,ns->pls", spread, virt_all, preferred_element_type=jnp.float32
    ).astype(jnp.bfloat16)
    layered = dressed.reshape(pieces, rows, 1, jpart, cols, ncol)
    returned = lax.all_to_all(
        lax.all_to_all(layered, "row", split_axis=1, concat_axis=0, tiled=True),
        "col",
        split_axis=4,
        concat_axis=2,
        tiled=True,
    )
    aligned = returned.reshape(pdev, mrow, ncol)
    theirs = swapped(screened, "aux", 0)
    with_mine = jnp.einsum("pls,qls->pq", aligned, screened, preferred_element_type=jnp.float32)
    with_theirs = jnp.einsum("pls,qls->pq", aligned, theirs, preferred_element_type=jnp.float32)
    first_half = jnp.where(aux_idx == 0, with_mine, with_theirs)
    second_half = jnp.where(aux_idx == 0, with_theirs, with_mine)
    partial_chi = jnp.concatenate([first_half, second_half], axis=1)
    total_chi = lax.psum(partial_chi, ("row", "col"))
    return total_chi / NAO


def solution(mesh):
    placed = (P("aux", "row", "col"), P("row", None), P("row", None), P())
    return jax.shard_map(
        shards, mesh=mesh, in_specs=placed, out_specs=P("aux", None), check_vma=False
    )
```

profile of v0, /device:TPU:0, one launch (start us, length us, event | category | flops | bytes accessed | tf_op | source)
XLA Modules:
  0.0 1038.5 jit_solution(6755601709993652313)
XLA Ops:
  6.5 0.7 all-gather.3.cloned.1.call-update
  7.3 0.7 all-gather.5.cloned.1.call-update
  8.0 0.9 fusion.13
  9.0 2.8 copy_multiply_fusion
  11.7 0.8 copy.15
  12.6 80.1 %all_to_all.66 = bf16[32,256,128]{2,1,0:T(8,128)(2,1)} all-to-all(bf16[32,256,128]{2,1,0:T(8,128)(2,1)S(1)} %copy.15), channel_id=1, replica_groups=mesh['aux'=2,'row'=8,'col'=16] {'row'}, dimensions={0} | all-to-all | bytes 4194304 | tf_op jit(solution)/shard_map/all_to_all | solution.py:33
  92.7 4.5 copy.16
  97.2 4.2 all_to_all.51
  101.4 45.5 %all-gather.3.cloned.1.call-done = bf16[2048,2048]{1,0:T(8,128)(2,1)} async-done(((bf16[256,2048]{1,0:T(8,128)(2,1)}), bf16[2048,2048]{1,0:T(8,128)(2,1)}) %all-gather.3.cloned.1.call-update) | async-done | bytes 8388624 | tf_op jit(solution)/shard_map/all_gather | solution.py:36
  146.9 9.8 fusion.10
  156.7 3.9 copy.17
  160.6 2.2 copy.18
  162.8 35.3 %all_to_all.67 = bf16[4,8,16,16,128]{4,3,1,0,2:T(8,128)(2,1)S(1)} all-to-all(bf16[4,8,16,16,128]{4,3,1,0,2:T(8,128)(2,1)S(1)} %copy.18), channel_id=1, replica_groups=mesh['aux'=2,'row'=8,'col'=16] {'col'}, dimensions={2} | all-to-all | bytes 4194304 | tf_op jit(solution)/shard_map/all_to_all | solution.py:44
  198.1 3.7 copy.19
  201.9 4.2 reshape.35
  206.0 35.8 %all-gather.5.cloned.1.call-done = bf16[2048,2048]{1,0:T(8,128)(2,1)} async-done(((bf16[256,2048]{1,0:T(8,128)(2,1)}), bf16[2048,2048]{1,0:T(8,128)(2,1)}) %all-gather.5.cloned.1.call-update) | async-done | bytes 8388624 | tf_op jit(solution)/shard_map/all_gather | solution.py:37
  241.9 8.5 fusion.7
  251.6 55.3 %all_to_all.68 = bf16[4,8,1,16,16,128]{5,4,3,0,2,1:T(8,128)(2,1)S(1)} all-to-all(bf16[4,8,1,16,16,128]{5,4,3,0,2,1:T(8,128)(2,1)S(1)} %copy.20), channel_id=1, replica_groups=mesh['aux'=2,'row'=8,'col'=16] {'row'}, dimensions={1} | all-to-all | bytes 4194304 | tf_op jit(solution)/shard_map/all_to_all | solution.py:51
  306.9 1.8 copy.21
  308.8 6.9 all-to-all-start.3
  315.7 27.9 %all-to-all-done.3 = bf16[32,1,1,16,16,128]{5,3,0,2,1,4:T(8,128)(2,1)} async-done(((bf16[32,1,1,16,16,128]{5,3,0,2,1,4:T(8,128)(2,1)}), bf16[32,1,1,16,16,128]{5,3,0,2,1,4:T(8,128)(2,1)}, u32[]{:S(2)}, u32[]{:S(2)}) %all-to-all-start.3) | async-done | bytes 2097184 | tf_op jit(solution)/shard_map/all_to_all | solution.py:50
  343.7 2.1 copy.22
  346.5 2.3 broadcast_select_fusion.1
  348.9 682.2 %psum.7 = f32[32,64]{1,0:T(8,128)S(1)} all-reduce(f32[32,64]{1,0:T(8,128)S(1)} %pad_maximum_fusion), channel_id=1, replica_groups=mesh['aux'=2,'row'=8,'col'=16] {'row','col'}, use_global_device_ids=true, to_apply=%region_0.1 | all-reduce | flops 2048 | bytes 16384 | tf_op jit(solution)/shard_map/psum | solution.py:64
  (10 shorter events, 2.8 us)
Async XLA Ops:
  6.5 140.3 %all-gather.3.cloned.1.call-start = ((), (), s32[]{:S(2)}) async-start(), calls=%async_computation.4 | async-start | bytes 9437184 | tf_op jit(solution)/shard_map/all_gather | solution.py:36
  7.3 234.6 %all-gather.5.cloned.1.call-start = ((), (), s32[]{:S(2)}) async-start(), calls=%async_computation.5 | async-start | bytes 9437184 | tf_op jit(solution)/shard_map/all_gather | solution.py:37
  308.8 34.9 %all-to-all-start.3 = ((bf16[32,1,1,16,16,128]{5,3,0,2,1,4:T(8,128)(2,1)}), bf16[32,1,1,16,16,128]{5,3,0,2,1,4:T(8,128)(2,1)}, u32[]{:S(2)}, u32[]{:S(2)}) async-start(bf16[32,1,1,16,16,128]{5,3,0,2,1,4:T(8,128)(2,1)} %copy.21), calls=%async_computation.3 | async-start | bytes 4194304 | tf_op jit(solution)/shard_map/all_to_all | solution.py:50
  315.6 30.8 %collective-permute-start = (bf16[32,256,128]{2,0,1:T(8,128)(2,1)S(1)}, bf16[32,256,128]{2,0,1:T(8,128)(2,1)}, u32[]{:S(2)}, u32[]{:S(2)}) collective-permute-start(bf16[32,256,128]{2,0,1:T(8,128)(2,1)S(1)} %copy_multiply_fusion), channel_id=1, source_target_pairs={{0,128},{128,0},{1,129},{129,1},{2,130},{130,2},{3,131},{131,3},{4... | collective-permute-start | bytes 6291464 | tf_op jit(solution)/shard_map/ppermute | solution.py:13
Sparse Core Ops, SparseCore 0:
  9.1 137.6 all-gather.2
  148.7 93.1 all-gather.4
where the time goes:
time: 1040 us
  blocking collectives  853 us (82%)
  waiting for transfers between devices  111 us (11%)
  local copies, waits for them, and re-layouts  28.8 us (3%)
  matrix products  21.3 us (2%)
  between operations  13.5 us (1%)
    psum x1, blocking collectives, shards(): total_chi = lax.psum(partial_chi, ('row', 'col'))  682 us
    all_to_all x1, blocking collectives, shards(): lax.all_to_all(screened, 'row', split_axis=0, concat_axis=1, tiled=True)  80.1 us
    all_to_all x1, blocking collectives, shards(): lax.all_to_all(layered, 'row', split_axis=1, concat_axis=0, tiled=True)  55.3 us
    all_gather x1, waiting for transfers between devices, shards(): lax.all_gather(occupied, 'row', axis=0, tiled=True)  45.5 us
    all_gather x1, waiting for transfers between devices, shards(): lax.all_gather(virtual, 'row', axis=0, tiled=True)  35.8 us
    all_to_all x1, blocking collectives, shards(): lax.all_to_all(shaped, 'col', split_axis=2, concat_axis=4, tiled=True)  35.3 us
    all_to_all x1, waiting for transfers between devices, shards(): lax.all_to_all(lax.all_to_all(layered, 'row', split_axis=1, concat_axis=0...  27.9 us
  transfers between devices with their start and end apart: 4, of which 3 were waited for; matrix products, arithmetic and copies ran while one was open for 3% of the time, Pallas kernels for 0%

commit v1 on v0

--- a/solution.py
+++ b/solution.py
@@ -61,7 +61,7 @@
     first_half = jnp.where(aux_idx == 0, with_mine, with_theirs)
     second_half = jnp.where(aux_idx == 0, with_theirs, with_mine)
     partial_chi = jnp.concatenate([first_half, second_half], axis=1)
-    total_chi = lax.psum(partial_chi, ("row", "col"))
+    total_chi = lax.psum(lax.psum(partial_chi, "col"), "row")
     return total_chi / NAO
 
 

time: 1040 us -> 455 us (0.44)
  blocking collectives: 853 us -> 269 us
    psum x1 -> x2, blocking collectives: 682 us -> 98.3 us  [shards(): total_chi = lax.psum(lax.psum(partial_chi, 'col'), 'row')]
  transfers between devices with their start and end apart: 4 -> 4, of which waited for: 3 -> 3; matrix products, arithmetic and copies ran while one was open for 3% -> 8% of each run, Pallas kernels for 0% -> 0%
where the time goes in v1:
time: 455 us
  blocking collectives  269 us (59%)
  waiting for transfers between devices  111 us (24%)
  local copies, waits for them, and re-layouts  28.8 us (6%)
  matrix products  21.3 us (5%)
  between operations  13.5 us (3%)
  starting transfers between devices  6.99 us (2%)
    psum x2, blocking collectives, shards(): total_chi = lax.psum(lax.psum(partial_chi, 'col'), 'row')  98.3 us
    all_to_all x1, blocking collectives, shards(): lax.all_to_all(screened, 'row', split_axis=0, concat_axis=1, tiled=True)  80.1 us
    all_to_all x1, blocking collectives, shards(): lax.all_to_all(layered, 'row', split_axis=1, concat_axis=0, tiled=True)  55.3 us
    all_gather x1, waiting for transfers between devices, shards(): lax.all_gather(occupied, 'row', axis=0, tiled=True)  45.5 us
    all_gather x1, waiting for transfers between devices, shards(): lax.all_gather(virtual, 'row', axis=0, tiled=True)  35.7 us
    all_to_all x1, blocking collectives, shards(): lax.all_to_all(shaped, 'col', split_axis=2, concat_axis=4, tiled=True)  35.4 us
    all_to_all x1, waiting for transfers between devices, shards(): lax.all_to_all(lax.all_to_all(layered, 'row', split_axis=1, concat_axis=0...  27.9 us
    dot_general x1, matrix products, shards(): jnp.einsum('ml,pmn->pln', occ_all, moved, preferred_element_type=jnp.floa...  9.81 us
  transfers between devices with their start and end apart: 4, of which 3 were waited for; matrix products, arithmetic and copies ran while one was open for 8% of the time, Pallas kernels for 0%

profile of v1, /device:TPU:0, one launch (start us, length us, event | category | flops | bytes accessed | tf_op | source)
XLA Modules:
  0.0 454.6 jit_solution(13387646627564546708)
XLA Ops:
  6.5 0.7 all-gather.3.cloned.1.call-update
  8.0 0.9 fusion.13
  9.0 2.8 copy_multiply_fusion
  11.7 0.8 copy.15
  12.6 80.1 %all_to_all.66 = bf16[32,256,128]{2,1,0:T(8,128)(2,1)} all-to-all(bf16[32,256,128]{2,1,0:T(8,128)(2,1)S(1)} %copy.15), channel_id=1, replica_groups=mesh['aux'=2,'row'=8,'col'=16] {'row'}, dimensions={0} | all-to-all | bytes 4194304 | tf_op jit(solution)/shard_map/all_to_all | solution.py:33
  92.7 4.5 copy.16
  97.2 4.2 all_to_all.51
  101.4 45.5 %all-gather.3.cloned.1.call-done = bf16[2048,2048]{1,0:T(8,128)(2,1)} async-done(((bf16[256,2048]{1,0:T(8,128)(2,1)}), bf16[2048,2048]{1,0:T(8,128)(2,1)}) %all-gather.3.cloned.1.call-update) | async-done | bytes 8388624 | tf_op jit(solution)/shard_map/all_gather | solution.py:36
  146.9 9.8 %fusion.10 = bf16[4,2048,128]{1,2,0:T(8,128)(2,1)} fusion(bf16[4,2048,128]{1,2,0:T(8,128)(2,1)} %all_to_all.51, bf16[2048,2048]{1,0:T(8,128)(2,1)} %all-gather.3.cloned.1.call-done), kind=kOutput, calls=%fused_computation.6 | convolution fusion | flops 4296015872 | bytes 12582912 | tf_op jit(solution)/shard_map/ml,pmn->pln/dot_general | solution.py:39
  156.7 3.9 copy.17
  160.6 2.2 copy.18
  162.8 35.4 %all_to_all.67 = bf16[4,8,16,16,128]{4,3,1,0,2:T(8,128)(2,1)S(1)} all-to-all(bf16[4,8,16,16,128]{4,3,1,0,2:T(8,128)(2,1)S(1)} %copy.18), channel_id=1, replica_groups=mesh['aux'=2,'row'=8,'col'=16] {'col'}, dimensions={2} | all-to-all | bytes 4194304 | tf_op jit(solution)/shard_map/all_to_all | solution.py:44
  198.2 3.7 copy.19
  202.0 4.2 reshape.35
  206.2 35.7 %all-gather.5.cloned.1.call-done = bf16[2048,2048]{1,0:T(8,128)(2,1)} async-done(((bf16[256,2048]{1,0:T(8,128)(2,1)}), bf16[2048,2048]{1,0:T(8,128)(2,1)}) %all-gather.5.cloned.1.call-update) | async-done | bytes 8388624 | tf_op jit(solution)/shard_map/all_gather | solution.py:37
  241.9 8.5 %fusion.7 = bf16[4,128,2048]{2,1,0:T(8,128)(2,1)S(1)} fusion(bf16[4,128,2048]{2,1,0:T(8,128)(2,1)} %reshape.35, bf16[2048,2048]{1,0:T(8,128)(2,1)} %all-gather.5.cloned.1.call-done), kind=kOutput, calls=%fused_computation.5 | convolution fusion | flops 4296015872 | bytes 12582912 | tf_op jit(solution)/shard_map/pln,ns->pls/dot_general | solution.py:46
  251.6 55.3 %all_to_all.68 = bf16[4,8,1,16,16,128]{5,4,3,0,2,1:T(8,128)(2,1)S(1)} all-to-all(bf16[4,8,1,16,16,128]{5,4,3,0,2,1:T(8,128)(2,1)S(1)} %copy.20), channel_id=1, replica_groups=mesh['aux'=2,'row'=8,'col'=16] {'row'}, dimensions={1} | all-to-all | bytes 4194304 | tf_op jit(solution)/shard_map/all_to_all | solution.py:51
  306.9 1.8 copy.21
  308.8 6.9 %all-to-all-start.3 = ((bf16[32,1,1,16,16,128]{5,3,0,2,1,4:T(8,128)(2,1)}), bf16[32,1,1,16,16,128]{5,3,0,2,1,4:T(8,128)(2,1)}, u32[]{:S(2)}, u32[]{:S(2)}) async-start(bf16[32,1,1,16,16,128]{5,3,0,2,1,4:T(8,128)(2,1)} %copy.21), calls=%async_computation.3 | async-start | bytes 4194304 | tf_op jit(solution)/shard_map/all_to_all | solution.py:50
  315.7 27.9 %all-to-all-done.3 = bf16[32,1,1,16,16,128]{5,3,0,2,1,4:T(8,128)(2,1)} async-done(((bf16[32,1,1,16,16,128]{5,3,0,2,1,4:T(8,128)(2,1)}), bf16[32,1,1,16,16,128]{5,3,0,2,1,4:T(8,128)(2,1)}, u32[]{:S(2)}, u32[]{:S(2)}) %all-to-all-start.3) | async-done | bytes 2097184 | tf_op jit(solution)/shard_map/all_to_all | solution.py:50
  343.7 2.1 copy.22
  346.5 2.3 broadcast_select_fusion.1
  348.9 70.5 %psum.14 = f32[32,64]{1,0:T(8,128)S(1)} all-reduce(f32[32,64]{1,0:T(8,128)S(1)} %pad_maximum_fusion), channel_id=1, replica_groups=mesh['aux'=2,'row'=8,'col'=16] {'col'}, use_global_device_ids=true, to_apply=%region_0.1 | all-reduce | flops 2048 | bytes 16384 | tf_op jit(solution)/shard_map/psum | solution.py:64
  419.4 27.7 %psum.15 = f32[32,64]{1,0:T(8,128)S(1)} all-reduce(f32[32,64]{1,0:T(8,128)S(1)} %psum.14), channel_id=1, replica_groups=mesh['aux'=2,'row'=8,'col'=16] {'row'}, use_global_device_ids=true, to_apply=%region_1.2 | all-reduce | flops 2048 | bytes 16384 | tf_op jit(solution)/shard_map/psum | solution.py:64
  (11 shorter events, 3.5 us)
Async XLA Ops:
  6.5 140.3 %all-gather.3.cloned.1.call-start = ((), (), s32[]{:S(2)}) async-start(), calls=%async_computation.4 | async-start | bytes 9437184 | tf_op jit(solution)/shard_map/all_gather | solution.py:36
  7.3 234.6 %all-gather.5.cloned.1.call-start = ((), (), s32[]{:S(2)}) async-start(), calls=%async_computation.5 | async-start | bytes 9437184 | tf_op jit(solution)/shard_map/all_gather | solution.py:37
  308.8 34.9 %all-to-all-start.3 = ((bf16[32,1,1,16,16,128]{5,3,0,2,1,4:T(8,128)(2,1)}), bf16[32,1,1,16,16,128]{5,3,0,2,1,4:T(8,128)(2,1)}, u32[]{:S(2)}, u32[]{:S(2)}) async-start(bf16[32,1,1,16,16,128]{5,3,0,2,1,4:T(8,128)(2,1)} %copy.21), calls=%async_computation.3 | async-start | bytes 4194304 | tf_op jit(solution)/shard_map/all_to_all | solution.py:50
  315.6 30.8 %collective-permute-start = (bf16[32,256,128]{2,0,1:T(8,128)(2,1)S(1)}, bf16[32,256,128]{2,0,1:T(8,128)(2,1)}, u32[]{:S(2)}, u32[]{:S(2)}) collective-permute-start(bf16[32,256,128]{2,0,1:T(8,128)(2,1)S(1)} %copy_multiply_fusion), channel_id=1, source_target_pairs={{0,128},{128,0},{1,129},{129,1},{2,130},{130,2},{3,131},{131,3},{4... | collective-permute-start | bytes 6291464 | tf_op jit(solution)/shard_map/ppermute | solution.py:13
Sparse Core Ops, SparseCore 0:
  9.1 137.6 all-gather.2
  148.7 93.1 all-gather.4

commit v2 on v0

--- a/solution.py
+++ b/solution.py
@@ -61,7 +61,7 @@
     first_half = jnp.where(aux_idx == 0, with_mine, with_theirs)
     second_half = jnp.where(aux_idx == 0, with_theirs, with_mine)
     partial_chi = jnp.concatenate([first_half, second_half], axis=1)
-    total_chi = lax.psum(partial_chi, ("row", "col"))
+    total_chi = jnp.sum(lax.all_gather(partial_chi, ("row", "col")), axis=0)
     return total_chi / NAO
 
 

time: 1040 us -> 470 us (0.45)
  blocking collectives: 853 us -> 171 us
  waiting for transfers between devices: 111 us -> 219 us
    psum x1 -> x0, blocking collectives: 682 us -> none  [shards(): total_chi = lax.psum(partial_chi, ('row', 'col'))]
    all_gather x0 -> x1, waiting for transfers between devices: none -> 109 us  [shards(): total_chi = jnp.sum(lax.all_gather(partial_chi, ('row', 'col')), axis=0)]
  transfers between devices with their start and end apart: 4 -> 5, of which waited for: 3 -> 4; matrix products, arithmetic and copies ran while one was open for 3% -> 8% of each run, Pallas kernels for 0% -> 0%
where the time goes in v2:
time: 470 us; the launch traced here: 467 us
  waiting for transfers between devices  219 us (47%)
  blocking collectives  171 us (36%)
  local copies, waits for them, and re-layouts  28.9 us (6%)
  matrix products  21.3 us (5%)
  between operations  13.2 us (3%)
  starting transfers between devices  7.03 us (1%)
  other arithmetic  6.74 us (1%)
    all_gather x1, waiting for transfers between devices, shards(): total_chi = jnp.sum(lax.all_gather(partial_chi, ('row', 'col')), axis=0)  109 us
    all_to_all x1, blocking collectives, shards(): lax.all_to_all(screened, 'row', split_axis=0, concat_axis=1, tiled=True)  80.1 us
    all_to_all x1, blocking collectives, shards(): lax.all_to_all(layered, 'row', split_axis=1, concat_axis=0, tiled=True)  55.3 us
    all_gather x1, waiting for transfers between devices, shards(): lax.all_gather(occupied, 'row', axis=0, tiled=True)  45.5 us
    all_gather x1, waiting for transfers between devices, shards(): lax.all_gather(virtual, 'row', axis=0, tiled=True)  35.7 us
    all_to_all x1, blocking collectives, shards(): lax.all_to_all(shaped, 'col', split_axis=2, concat_axis=4, tiled=True)  35.4 us
    all_to_all x1, waiting for transfers between devices, shards(): lax.all_to_all(lax.all_to_all(layered, 'row', split_axis=1, concat_axis=0...  27.9 us
    dot_general x1, matrix products, shards(): jnp.einsum('ml,pmn->pln', occ_all, moved, preferred_element_type=jnp.floa...  9.82 us
  transfers between devices with their start and end apart: 5, of which 4 were waited for; matrix products, arithmetic and copies ran while one was open for 8% of the time, Pallas kernels for 0%

profile of v2, /device:TPU:0, one launch (start us, length us, event | category | flops | bytes accessed | tf_op | source)
XLA Modules:
  0.0 467.1 jit_solution(16406083937011497203)
XLA Ops:
  6.5 0.7 all-gather.5.cloned.1.call-update
  8.0 0.9 fusion.13
  9.0 2.8 copy_multiply_fusion
  11.7 0.8 copy.15
  12.6 80.1 %all_to_all.66 = bf16[32,256,128]{2,1,0:T(8,128)(2,1)} all-to-all(bf16[32,256,128]{2,1,0:T(8,128)(2,1)S(1)} %copy.15), channel_id=1, replica_groups=mesh['aux'=2,'row'=8,'col'=16] {'row'}, dimensions={0} | all-to-all | bytes 4194304 | tf_op jit(solution)/shard_map/all_to_all | solution.py:33
  92.7 4.5 copy.16
  97.2 4.2 all_to_all.51
  101.4 45.5 %all-gather.5.cloned.1.call-done = bf16[2048,2048]{1,0:T(8,128)(2,1)} async-done(((bf16[256,2048]{1,0:T(8,128)(2,1)}), bf16[2048,2048]{1,0:T(8,128)(2,1)}) %all-gather.5.cloned.1.call-update) | async-done | bytes 8388624 | tf_op jit(solution)/shard_map/all_gather | solution.py:36
  146.9 9.8 %fusion.10 = bf16[4,2048,128]{1,2,0:T(8,128)(2,1)} fusion(bf16[4,2048,128]{1,2,0:T(8,128)(2,1)} %all_to_all.51, bf16[2048,2048]{1,0:T(8,128)(2,1)} %all-gather.5.cloned.1.call-done), kind=kOutput, calls=%fused_computation.6 | convolution fusion | flops 4296015872 | bytes 12582912 | tf_op jit(solution)/shard_map/ml,pmn->pln/dot_general | solution.py:39
  156.7 4.0 copy.17
  160.6 2.2 copy.18
  162.8 35.4 %all_to_all.67 = bf16[4,8,16,16,128]{4,3,1,0,2:T(8,128)(2,1)S(1)} all-to-all(bf16[4,8,16,16,128]{4,3,1,0,2:T(8,128)(2,1)S(1)} %copy.18), channel_id=1, replica_groups=mesh['aux'=2,'row'=8,'col'=16] {'col'}, dimensions={2} | all-to-all | bytes 4194304 | tf_op jit(solution)/shard_map/all_to_all | solution.py:44
  198.3 3.8 copy.19
  202.0 4.2 reshape.35
  206.2 35.7 %all-gather.7.cloned.1.call-done = bf16[2048,2048]{1,0:T(8,128)(2,1)} async-done(((bf16[256,2048]{1,0:T(8,128)(2,1)}), bf16[2048,2048]{1,0:T(8,128)(2,1)}) %all-gather.7.cloned.1.call-update) | async-done | bytes 8388624 | tf_op jit(solution)/shard_map/all_gather | solution.py:37
  241.9 8.5 %fusion.7 = bf16[4,128,2048]{2,1,0:T(8,128)(2,1)S(1)} fusion(bf16[4,128,2048]{2,1,0:T(8,128)(2,1)} %reshape.35, bf16[2048,2048]{1,0:T(8,128)(2,1)} %all-gather.7.cloned.1.call-done), kind=kOutput, calls=%fused_computation.5 | convolution fusion | flops 4296015872 | bytes 12582912 | tf_op jit(solution)/shard_map/pln,ns->pls/dot_general | solution.py:46
  251.6 55.3 %all_to_all.68 = bf16[4,8,1,16,16,128]{5,4,3,0,2,1:T(8,128)(2,1)S(1)} all-to-all(bf16[4,8,1,16,16,128]{5,4,3,0,2,1:T(8,128)(2,1)S(1)} %copy.20), channel_id=1, replica_groups=mesh['aux'=2,'row'=8,'col'=16] {'row'}, dimensions={1} | all-to-all | bytes 4194304 | tf_op jit(solution)/shard_map/all_to_all | solution.py:51
  306.9 1.9 copy.21
  308.8 6.9 %all-to-all-start.3 = ((bf16[32,1,1,16,16,128]{5,3,0,2,1,4:T(8,128)(2,1)}), bf16[32,1,1,16,16,128]{5,3,0,2,1,4:T(8,128)(2,1)}, u32[]{:S(2)}, u32[]{:S(2)}) async-start(bf16[32,1,1,16,16,128]{5,3,0,2,1,4:T(8,128)(2,1)} %copy.21), calls=%async_computation.3 | async-start | bytes 4194304 | tf_op jit(solution)/shard_map/all_to_all | solution.py:50
  315.8 27.9 %all-to-all-done.3 = bf16[32,1,1,16,16,128]{5,3,0,2,1,4:T(8,128)(2,1)} async-done(((bf16[32,1,1,16,16,128]{5,3,0,2,1,4:T(8,128)(2,1)}), bf16[32,1,1,16,16,128]{5,3,0,2,1,4:T(8,128)(2,1)}, u32[]{:S(2)}, u32[]{:S(2)}) %all-to-all-start.3) | async-done | bytes 2097184 | tf_op jit(solution)/shard_map/all_to_all | solution.py:50
  343.7 2.1 copy.22
  346.5 2.3 broadcast_select_fusion.1
  349.5 108.7 %all-gather.9.cloned.1.call-done = f32[4096,64]{1,0:T(8,128)} async-done(((f32[32,64]{1,0:T(8,128)}), f32[4096,64]{1,0:T(8,128)}) %all-gather.9.cloned.1.call-update) | async-done | bytes 1048592 | tf_op jit(solution)/shard_map/all_gather | solution.py:64
  458.2 1.8 reduce_sum.9
  (13 shorter events, 4.1 us)
Async XLA Ops:
  6.5 140.3 %all-gather.5.cloned.1.call-start = ((), (), s32[]{:S(2)}) async-start(), calls=%async_computation.4 | async-start | bytes 9437184 | tf_op jit(solution)/shard_map/all_gather | solution.py:36
  7.3 234.6 %all-gather.7.cloned.1.call-start = ((), (), s32[]{:S(2)}) async-start(), calls=%async_computation.5 | async-start | bytes 9437184 | tf_op jit(solution)/shard_map/all_gather | solution.py:37
  308.8 34.9 %all-to-all-start.3 = ((bf16[32,1,1,16,16,128]{5,3,0,2,1,4:T(8,128)(2,1)}), bf16[32,1,1,16,16,128]{5,3,0,2,1,4:T(8,128)(2,1)}, u32[]{:S(2)}, u32[]{:S(2)}) async-start(bf16[32,1,1,16,16,128]{5,3,0,2,1,4:T(8,128)(2,1)} %copy.21), calls=%async_computation.3 | async-start | bytes 4194304 | tf_op jit(solution)/shard_map/all_to_all | solution.py:50
  315.6 142.5 %all-gather.9.cloned.1.call-start = ((), (), s32[]{:S(2)}) async-start(), calls=%async_computation.6 | async-start | bytes 2113536 | tf_op jit(solution)/shard_map/all_gather | solution.py:64
  315.7 30.8 %collective-permute-start = (bf16[32,256,128]{2,0,1:T(8,128)(2,1)S(1)}, bf16[32,256,128]{2,0,1:T(8,128)(2,1)}, u32[]{:S(2)}, u32[]{:S(2)}) collective-permute-start(bf16[32,256,128]{2,0,1:T(8,128)(2,1)S(1)} %copy_multiply_fusion), channel_id=1, source_target_pairs={{0,128},{128,0},{1,129},{129,1},{2,130},{130,2},{3,131},{131,3},{4... | collective-permute-start | bytes 6291464 | tf_op jit(solution)/shard_map/ppermute | solution.py:13
Sparse Core Ops, SparseCore 0:
  9.1 137.6 all-gather.4
  148.7 93.1 all-gather.6
  349.6 108.4 all-gather.8
